TPU v7x, 32 devices: a whole 2x2x4 slice. The times are simulated.
32 devices in a mesh: row: 2 (over x), col: 16 (over z, y, core).
Axes of the slice: x: 2, y: 2, z: 4, core: 2. Of those that a mesh axis runs over, the one named last changes fastest.
Arguments:
- features: bfloat16 [64, 768, 256], P('row', 'col'), may hold values from -6 to 6
- conv_one: bfloat16 [3, 3, 256, 256], replicated, may hold values from -0.125 to 0.125
- bias_one: float32 [256], replicated, may hold values from -3 to 3
- conv_two: bfloat16 [3, 3, 256, 512], replicated, may hold values from -0.125 to 0.125
- bias_two: float32 [512], replicated, may hold values from -3 to 3
- conv_three: bfloat16 [16, 3, 3, 32, 32], P('col'), may hold values from -0.375 to 0.375
- bias_three: float32 [512], P('col'), may hold values from -3 to 3
Outputs:
- encoded: bfloat16 [32, 512, 384], P('row', 'col')
All inputs are finite; a program needn't handle non-finite values.
Results may differ from a plain program's by a relative error of at most 0.0051.
Values may be sent and summed in bfloat16 or wider, within the bound.
A program may use at most 64 MiB of HBM per device.

v0:
```python
import jax
import jax.numpy as jnp
from jax import lax
from jax.sharding import PartitionSpec as P


def padded_2(block, sides, width):
    for axis, dim in sides:
        count = lax.axis_size(axis)
        forward = [(i, i + 1) for i in range(count - 1)]
        backward = [(target, source) for source, target in forward]
        low = lax.ppermute(
            lax.slice_in_dim(block, block.shape[dim] - width, None, axis=dim), axis, forward
        )
        high = lax.ppermute(lax.slice_in_dim(block, 0, width, axis=dim), axis, backward)
        block = jnp.concatenate([low, block, high], axis=dim)
    return block


def passed_along(block, axis, distance):
    devices = range(lax.axis_size(axis))
    route = [(i - distance, i) for i in devices if i - distance in devices]
    return lax.ppermute(block, axis, route)


def conv_taps(padded, weight, out_rows, out_cols, stride):
    summed = None
    for tap_row in range(3):
        for tap_col in range(3):
            window = lax.slice(
                padded,
                (tap_row, tap_col, 0),
                (
                    tap_row + stride * (out_rows - 1) + 1,
                    tap_col + stride * (out_cols - 1) + 1,
                    padded.shape[2],
                ),
                (stride, stride, 1),
            )
            product = jnp.dot(
                window.reshape(out_rows * out_cols, padded.shape[2]),
                weight[tap_row, tap_col],
                preferred_element_type=jnp.float32,
            )
            summed = product if summed is None else summed + product
    return summed.reshape(out_rows, out_cols, weight.shape[3])


def on_device(features, conv_one, bias_one, conv_two, bias_two, conv_three, bias_three):
    tile_rows = features.shape[0]
    tile_cols = features.shape[1]
    padded = padded_2(features, (("row", 0), ("col", 1)), 1)
    summed = conv_taps(padded, conv_one, tile_rows, tile_cols, 1)
    layer_one = jax.nn.relu(summed + bias_one).astype(jnp.bfloat16)
    upper_row = passed_along(layer_one[tile_rows - 1 :], "row", 1)
    extended = jnp.concatenate([upper_row, layer_one], 0)
    left_column = passed_along(extended[:, tile_cols - 1 :], "col", 1)
    extended = jnp.concatenate([left_column, extended], 1)
    summed = conv_taps(extended, conv_two, tile_rows // 2, tile_cols // 2, 2)
    layer_two = jax.nn.relu(summed + bias_two).astype(jnp.bfloat16)
    grouped = lax.all_to_all(layer_two, "col", split_axis=2, concat_axis=1, tiled=True)
    grouped = padded_2(grouped, (("row", 0),), 1)
    grouped = jnp.pad(grouped, ((0, 0), (1, 1), (0, 0)))
    local_groups = conv_three.shape[0]
    group_width = conv_three.shape[3]
    out_rows = layer_two.shape[0]
    full_cols = grouped.shape[1] - 2
    summed = None
    for tap_row in range(3):
        for tap_col in range(3):
            window = grouped[tap_row : tap_row + out_rows, tap_col : tap_col + full_cols].reshape(
                out_rows, full_cols, local_groups, group_width
            )
            product = jnp.einsum(
                "rwgi,gio->rgow",
                window,
                conv_three[:, tap_row, tap_col],
                preferred_element_type=jnp.float32,
            )
            summed = product if summed is None else summed + product
    result = (
        summed.reshape(out_rows, local_groups * group_width, full_cols) + bias_three[None, :, None]
    )
    return result.astype(jnp.bfloat16)


def solution(mesh):
    in_specs = (
        P("row", "col", None),
        P(),
        P(),
        P(),
        P(),
        P("col", None, None, None, None),
        P("col"),
    )
    out_specs = P("row", "col", None)
    return jax.shard_map(
        on_device, mesh=mesh, in_specs=in_specs, out_specs=out_specs, check_vma=False
    )
```

profile of v0, /device:TPU:0, one launch (start us, length us, event | category | flops | bytes accessed | tf_op | source)
XLA Modules:
  0.0 93.5 jit_solution(4920264722464064641)
XLA Ops:
  0.0 0.8 fusion.89
  0.8 4.9 %collective-permute-start = (bf16[1,48,256]{2,1,0:T(8,128)(2,1)S(1)}, bf16[1,48,256]{2,1,0:T(8,128)(2,1)S(1)}, u32[]{:S(2)}, u32[]{:S(2)}) collective-permute-start(bf16[1,48,256]{2,1,0:T(8,128)(2,1)S(1)} %get-tuple-element.22), channel_id=1, source_target_pairs={{0,16},{1,17},{2,18},{3,19},{4,20},{5,21},{6,22},{7,23},{8,24},{9,... | collective-permute-start | bytes 73736 | tf_op jit(solution)/shard_map/ppermute | solution.py:12
  5.6 1.3 %collective-permute-start.1 = (bf16[1,48,256]{2,1,0:T(8,128)(2,1)S(1)}, bf16[1,48,256]{2,1,0:T(8,128)(2,1)S(1)}, u32[]{:S(2)}, u32[]{:S(2)}) collective-permute-start(bf16[1,48,256]{2,1,0:T(8,128)(2,1)S(1)} %get-tuple-element.21), channel_id=1, source_target_pairs={{16,0},{17,1},{18,2},{19,3},{20,4},{21,5},{22,6},{23,7},{24,8},{25... | collective-permute-start | bytes 73736 | tf_op jit(solution)/shard_map/ppermute | solution.py:15
  6.9 0.2 collective-permute-done
  7.1 4.2 %collective-permute-done.1 = bf16[1,48,256]{2,1,0:T(8,128)(2,1)S(1)} collective-permute-done((bf16[1,48,256]{2,1,0:T(8,128)(2,1)S(1)}, bf16[1,48,256]{2,1,0:T(8,128)(2,1)S(1)}, u32[]{:S(2)}, u32[]{:S(2)}) %collective-permute-start.1) | collective-permute-done | bytes 24608 | tf_op jit(solution)/shard_map/ppermute | solution.py:15
  11.3 2.2 %pad_maximum_fusion.4 = (bf16[32,48,256]{2,1,0:T(8,128)(2,1)S(1)}, bf16[32,48,256]{2,1,0:T(8,128)(2,1)S(1)}, bf16[34,48,256]{2,1,0:T(8,128)(2,1)S(1)}) fusion(bf16[32,48,256]{2,1,0:T(8,128)(2,1)} %param.7, bf16[1,48,256]{2,1,0:T(8,128)(2,1)S(1)} %collective-permute-done, bf16[1,48,256]{2,1,0:T(8,128)(2,1)S(1)} %collective-permute-done.1, ...), kind=kLoop, calls=%fused_computation.49 | loop fusion | flops 3145728 | bytes 3194880 | tf_op jit(solution)/shard_map/concatenate | solution.py:16
  13.6 1.3 %collective-permute-start.2 = (bf16[34,1,256]{2,1,0:T(2,128)(2,1)S(1)}, bf16[34,1,256]{2,1,0:T(2,128)(2,1)S(1)}, u32[]{:S(2)}, u32[]{:S(2)}) collective-permute-start(bf16[34,1,256]{2,1,0:T(2,128)(2,1)S(1)} %get-tuple-element.16), channel_id=1, source_target_pairs={{0,1},{1,2},{2,3},{3,4},{4,5},{5,6},{6,7},{7,8},{8,9},{9,10},{10,1... | collective-permute-start | bytes 52232 | tf_op jit(solution)/shard_map/ppermute | solution.py:12
  14.9 1.3 %collective-permute-start.3 = (bf16[34,1,256]{2,1,0:T(2,128)(2,1)S(1)}, bf16[34,1,256]{2,1,0:T(2,128)(2,1)S(1)}, u32[]{:S(2)}, u32[]{:S(2)}) collective-permute-start(bf16[34,1,256]{2,1,0:T(2,128)(2,1)S(1)} %get-tuple-element.17), channel_id=1, source_target_pairs={{1,0},{2,1},{3,2},{4,3},{5,4},{6,5},{7,6},{8,7},{9,8},{10,9},{11,1... | collective-permute-start | bytes 52232 | tf_op jit(solution)/shard_map/ppermute | solution.py:15
  16.2 0.4 fusion.54
  16.6 0.4 fusion.47
  17.0 2.8 %collective-permute-done.3 = bf16[34,1,256]{2,1,0:T(2,128)(2,1)S(1)} collective-permute-done((bf16[34,1,256]{2,1,0:T(2,128)(2,1)S(1)}, bf16[34,1,256]{2,1,0:T(2,128)(2,1)S(1)}, u32[]{:S(2)}, u32[]{:S(2)}) %collective-permute-start.3) | collective-permute-done | bytes 17440 | tf_op jit(solution)/shard_map/ppermute | solution.py:15
  19.8 2.9 %pad_maximum_fusion.3 = (bf16[32,48,256]{2,1,0:T(8,128)(2,1)S(1)}, bf16[32,48,256]{2,1,0:T(8,128)(2,1)S(1)}, bf16[32,48,256]{2,1,0:T(8,128)(2,1)S(1)}, bf16[32,4...) fusion(bf16[34,48,256]{2,1,0:T(8,128)(2,1)S(1)} %constant_dynamic-update-slice_fusion,, ...), kind=kLoop, calls=%fused_computation.48 | loop fusion | flops 9437184 | bytes 5588992 | tf_op jit(solution)/shard_map/concatenate | solution.py:16
  22.7 0.4 fusion.45
  23.1 0.4 convolution_add_fusion.5
  23.5 0.4 convolution_add_fusion.4
  23.8 0.4 convolution_add_fusion.3
  24.2 0.7 copy-done
  25.0 0.4 convolution_add_fusion.2
  25.3 0.4 convolution_add_fusion.1
  25.7 0.5 fusion.1
  26.4 0.2 maximum_convert_fusion
  26.6 1.6 %collective-permute-start.4 = (bf16[1,48,256]{2,1,0:T(8,128)(2,1)S(1)}, bf16[1,48,256]{2,1,0:T(8,128)(2,1)S(1)}, u32[]{:S(2)}, u32[]{:S(2)}) collective-permute-start(bf16[1,48,256]{2,1,0:T(8,128)(2,1)S(1)} %slice.272), channel_id=1, source_target_pairs={{0,16},{1,17},{2,18},{3,19},{4,20},{5,21},{6,22},{7,23},{8,24},{9,... | collective-permute-start | bytes 73736 | tf_op jit(solution)/shard_map/ppermute | solution.py:23
  28.2 0.5 slice.231
  28.8 0.5 slice.233
  29.3 0.9 slice.237
  30.1 0.9 slice.239
  31.1 4.3 %collective-permute-start.5 = (bf16[33,1,256]{2,1,0:T(2,128)(2,1)S(1)}, bf16[33,1,256]{2,1,0:T(2,128)(2,1)S(1)}, u32[]{:S(2)}, u32[]{:S(2)}) collective-permute-start(bf16[33,1,256]{2,1,0:T(2,128)(2,1)S(1)} %fusion.66), channel_id=1, source_target_pairs={{0,1},{1,2},{2,3},{3,4},{4,5},{5,6},{6,7},{7,8},{8,9},{9,10},{10,1... | collective-permute-start | bytes 50696 | tf_op jit(solution)/shard_map/ppermute | solution.py:23
  35.4 0.5 slice.225
  36.0 1.2 %fusion.33 = f32[384,512]{1,0:T(8,128)S(1)} fusion(bf16[384,256]{1,0:T(8,128)(2,1)S(1)} %bitcast.192, bf16[3,3,256,512]{3,2,1,0:T(8,128)(2,1)} %param.10), kind=kOutput, calls=%fused_computation.76 | convolution fusion | flops 100663296 | bytes 1245184 | tf_op jit(solution)/shard_map/dot_general | solution.py:40
  37.2 5.0 %slice.227 = bf16[16,24,256]{2,1,0:T(8,128)(2,1)} slice(bf16[33,48,256]{2,1,0:T(8,128)(2,1)S(1)} %pad_maximum_fusion), slice={[0:31:2], [1:48:2], [0:256:1]} | slice | bytes 393216 | tf_op jit(solution)/shard_map/slice | solution.py:30
  42.2 0.5 maximum_maximum_fusion
  42.7 0.5 slice.223
  43.2 0.5 slice.229
  43.7 0.7 slice.235
  44.5 1.4 %convolution_add_fusion.20 = f32[384,512]{1,0:T(8,128)S(1)} fusion(f32[384,512]{1,0:T(8,128)S(1)} %fusion.33, bf16[384,256]{1,0:T(8,128)(2,1)S(1)} %bitcast.200, bf16[3,3,256,512]{3,2,1,0:T(8,128)(2,1)} %param.10), kind=kOutput, calls=%fused_computation.32 | convolution fusion | flops 100859904 | bytes 2031616 | tf_op jit(solution)/shard_map/dot_general | solution.py:40
  45.9 1.2 %convolution_add_fusion.19 = f32[384,512]{1,0:T(8,128)S(1)} fusion(f32[384,512]{1,0:T(8,128)S(1)} %convolution_add_fusion.20, bf16[384,256]{1,0:T(8,128)(2,1)S(1)} %bitcast.197, bf16[3,3,256,512]{3,2,1,0:T(8,128)(2,1)} %param.10), kind=kOutput, calls=%fused_computation.31 | convolution fusion | flops 100859904 | bytes 2031616 | tf_op jit(solution)/shard_map/dot_general | solution.py:40
  47.1 0.3 convolution_add_fusion.18
  47.4 0.3 convolution_add_fusion.17
  47.6 0.3 convolution_add_fusion.16
  47.9 0.3 convolution_add_fusion.15
  48.2 0.3 convolution_add_fusion.14
  48.4 0.3 convolution_add_fusion.13
  48.9 2.0 %copy.53 = bf16[16,24,512]{1,0,2:T(8,128)(2,1)S(1)} copy(bf16[16,24,512]{2,1,0:T(8,128)(2,1)S(1)} %maximum_convert_fusion.1) | data formatting | bytes 786432 | tf_op jit(solution)/shard_map/convert_element_type | solution.py:60
  50.9 2.7 %reshape.188 = bf16[16,2,6144]{2,1,0:T(2,128)(2,1)S(1)} reshape(bf16[512,16,24]{2,1,0:T(8,128)(2,1)S(1)} %bitcast.179) | data formatting | bytes 786432
  53.6 17.8 %all_to_all.18 = bf16[16,2,6144]{2,1,0:T(2,128)(2,1)S(1)} all-to-all(bf16[16,2,6144]{2,1,0:T(2,128)(2,1)S(1)} %reshape.188), channel_id=1, replica_groups=mesh['row'=2,'col'=16] {'col'}, dimensions={0} | all-to-all | bytes 786432 | tf_op jit(solution)/shard_map/all_to_all | solution.py:61
  71.5 3.0 %reshape.189 = bf16[512,16,24]{2,1,0:T(8,128)(2,1)S(1)} reshape(bf16[16,2,6144]{2,1,0:T(2,128)(2,1)S(1)} %all_to_all.18) | data formatting | bytes 786432
  74.4 3.1 %copy.67 = bf16[16,24,16,32]{3,2,1,0:T(8,128)(2,1)} copy(bf16[16,24,16,32]{1,0,3,2:T(8,128)(2,1)S(1)} %bitcast.177) | data formatting | bytes 786432 | tf_op jit(solution)/shard_map/all_to_all | solution.py:61
  77.5 1.0 %fusion.87 = (bf16[1,16,24,32]{3,1,2,0:T(8,128)(2,1)S(1)}, bf16[1,16,24,32]{3,1,2,0:T(8,128)(2,1)S(1)}) fusion(bf16[16,16,24,32]{3,1,2,0:T(8,128)(2,1)} %bitcast.191), kind=kLoop, calls=%fused_computation.133 | loop fusion | bytes 98304 | tf_op jit(solution)/shard_map/slice | solution.py:13
  78.5 0.2 copy.55
  78.8 2.8 %collective-permute-start.6 = (bf16[1,384,32]{1,2,0:T(8,128)(2,1)S(1)}, bf16[1,384,32]{1,2,0:T(8,128)(2,1)S(1)}, u32[]{:S(2)}, u32[]{:S(2)}) collective-permute-start(bf16[1,384,32]{1,2,0:T(8,128)(2,1)S(1)} %slice.242), channel_id=1, source_target_pairs={{0,16},{1,17},{2,18},{3,19},{4,20},{5,21},{6,22},{7,23},{8,24},{9,... | collective-permute-start | bytes 73736 | tf_op jit(solution)/shard_map/ppermute | solution.py:12
  81.7 0.2 copy.57
  82.0 1.5 %collective-permute-start.7 = (bf16[1,384,32]{1,2,0:T(8,128)(2,1)S(1)}, bf16[1,384,32]{1,2,0:T(8,128)(2,1)S(1)}, u32[]{:S(2)}, u32[]{:S(2)}) collective-permute-start(bf16[1,384,32]{1,2,0:T(8,128)(2,1)S(1)} %slice.244), channel_id=1, source_target_pairs={{16,0},{17,1},{18,2},{19,3},{20,4},{21,5},{22,6},{23,7},{24,8},{25... | collective-permute-start | bytes 73736 | tf_op jit(solution)/shard_map/ppermute | solution.py:15
  83.5 2.7 %copy.56 = bf16[16,16,24,32]{2,1,3,0:T(8,128)(2,1)} copy(bf16[16,16,24,32]{2,0,3,1:T(8,128)(2,1)S(1)} %bitcast.178) | data formatting | bytes 786432 | tf_op jit(solution)/shard_map/all_to_all | solution.py:61
  86.2 3.4 %all_to_all.16 = bf16[16,384,32]{1,2,0:T(8,128)(2,1)S(1)} reshape(bf16[16,16,24,32]{2,1,3,0:T(8,128)(2,1)} %copy.56) | data formatting | bytes 786432 | tf_op jit(solution)/shard_map/all_to_all | solution.py:61
  89.7 0.3 fusion.15
  90.0 0.3 fusion.16
  90.3 0.3 fusion.23
  90.6 0.3 convolution_add_fusion.12
  90.9 0.3 convolution_add_fusion.11
  91.2 0.3 convolution_add_fusion.10
  91.5 0.3 convolution_add_fusion.9
  91.9 0.3 convolution_add_fusion.8
  92.2 0.3 convolution_add_fusion.7
  92.5 1.0 %fusion.5 = bf16[16,32,384]{2,1,0:T(8,128)(2,1)} fusion(f32[16,384,32]{1,2,0:T(8,128)S(1)} %fusion.16, f32[16,384,32]{1,2,0:T(8,128)S(1)} %convolution_add_fusion.7, bf16[1,384,32]{1,2,0:T(8,128)(2,1)S(1)} %collective-permute-done.7, bf16[16,384,32]{1,2,0:T(8,128)(2,1)S(1)} %all_to_all.16, f32[32]{0:T(128)S(1)} %copy-done.7, ...), kind=kOutput, calls=%fused_computation.33 | convolution fusion | flops 14155776 | bytes 2392576 | tf_op jit(solution)/shard_map/rwgi,gio->rgow/dot_general | solution.py:74
  (29 shorter events, 1.0 us)
Async XLA Ops:
  0.8 6.4 %collective-permute-start = (bf16[1,48,256]{2,1,0:T(8,128)(2,1)S(1)}, bf16[1,48,256]{2,1,0:T(8,128)(2,1)S(1)}, u32[]{:S(2)}, u32[]{:S(2)}) collective-permute-start(bf16[1,48,256]{2,1,0:T(8,128)(2,1)S(1)} %get-tuple-element.22), channel_id=1, source_target_pairs={{0,16},{1,17},{2,18},{3,19},{4,20},{5,21},{6,22},{7,23},{8,24},{9,... | collective-permute-start | bytes 73736 | tf_op jit(solution)/shard_map/ppermute | solution.py:12
  5.6 5.7 %collective-permute-start.1 = (bf16[1,48,256]{2,1,0:T(8,128)(2,1)S(1)}, bf16[1,48,256]{2,1,0:T(8,128)(2,1)S(1)}, u32[]{:S(2)}, u32[]{:S(2)}) collective-permute-start(bf16[1,48,256]{2,1,0:T(8,128)(2,1)S(1)} %get-tuple-element.21), channel_id=1, source_target_pairs={{16,0},{17,1},{18,2},{19,3},{20,4},{21,5},{22,6},{23,7},{24,8},{25... | collective-permute-start | bytes 73736 | tf_op jit(solution)/shard_map/ppermute | solution.py:15
  7.1 9.1 %copy-start.2 = (bf16[3,3,256,256]{3,2,1,0:T(8,128)(2,1)S(1)}, bf16[3,3,256,256]{3,2,1,0:T(8,128)(2,1)}, u32[]{:S(2)}) copy-start(bf16[3,3,256,256]{3,2,1,0:T(8,128)(2,1)} %param.8) | copy-start | bytes 3538948
  13.6 3.3 %collective-permute-start.2 = (bf16[34,1,256]{2,1,0:T(2,128)(2,1)S(1)}, bf16[34,1,256]{2,1,0:T(2,128)(2,1)S(1)}, u32[]{:S(2)}, u32[]{:S(2)}) collective-permute-start(bf16[34,1,256]{2,1,0:T(2,128)(2,1)S(1)} %get-tuple-element.16), channel_id=1, source_target_pairs={{0,1},{1,2},{2,3},{3,4},{4,5},{5,6},{6,7},{7,8},{8,9},{9,10},{10,1... | collective-permute-start | bytes 52232 | tf_op jit(solution)/shard_map/ppermute | solution.py:12
  14.9 4.9 %collective-permute-start.3 = (bf16[34,1,256]{2,1,0:T(2,128)(2,1)S(1)}, bf16[34,1,256]{2,1,0:T(2,128)(2,1)S(1)}, u32[]{:S(2)}, u32[]{:S(2)}) collective-permute-start(bf16[34,1,256]{2,1,0:T(2,128)(2,1)S(1)} %get-tuple-element.17), channel_id=1, source_target_pairs={{1,0},{2,1},{3,2},{4,3},{5,4},{6,5},{7,6},{8,7},{9,8},{10,9},{11,1... | collective-permute-start | bytes 52232 | tf_op jit(solution)/shard_map/ppermute | solution.py:15
  23.8 1.1 %copy-start = (bf16[32,48,256]{2,1,0:T(8,128)(2,1)S(1)}, bf16[32,48,256]{2,1,0:T(8,128)(2,1)}, u32[]{:S(2)}) copy-start(bf16[32,48,256]{2,1,0:T(8,128)(2,1)} %param.7) | copy-start | bytes 2359300
  25.7 0.7 copy-start.6
  26.6 4.4 %collective-permute-start.4 = (bf16[1,48,256]{2,1,0:T(8,128)(2,1)S(1)}, bf16[1,48,256]{2,1,0:T(8,128)(2,1)S(1)}, u32[]{:S(2)}, u32[]{:S(2)}) collective-permute-start(bf16[1,48,256]{2,1,0:T(8,128)(2,1)S(1)} %slice.272), channel_id=1, source_target_pairs={{0,16},{1,17},{2,18},{3,19},{4,20},{5,21},{6,22},{7,23},{8,24},{9,... | collective-permute-start | bytes 73736 | tf_op jit(solution)/shard_map/ppermute | solution.py:23
  31.1 11.1 %collective-permute-start.5 = (bf16[33,1,256]{2,1,0:T(2,128)(2,1)S(1)}, bf16[33,1,256]{2,1,0:T(2,128)(2,1)S(1)}, u32[]{:S(2)}, u32[]{:S(2)}) collective-permute-start(bf16[33,1,256]{2,1,0:T(2,128)(2,1)S(1)} %fusion.66), channel_id=1, source_target_pairs={{0,1},{1,2},{2,3},{3,4},{4,5},{5,6},{6,7},{7,8},{8,9},{9,10},{10,1... | collective-permute-start | bytes 50696 | tf_op jit(solution)/shard_map/ppermute | solution.py:23
  42.7 3.2 %copy-start.3 = (bf16[16,24,256]{2,1,0:T(8,128)(2,1)S(1)}, bf16[16,24,256]{2,1,0:T(8,128)(2,1)}, u32[]{:S(2)}) copy-start(bf16[16,24,256]{2,1,0:T(8,128)(2,1)} %slice.227) | copy-start | bytes 589828
  44.5 2.6 %copy-start.1 = (bf16[3,3,256,512]{3,2,1,0:T(8,128)(2,1)S(1)}, bf16[3,3,256,512]{3,2,1,0:T(8,128)(2,1)}, u32[]{:S(2)}) copy-start(bf16[3,3,256,512]{3,2,1,0:T(8,128)(2,1)} %param.10) | copy-start | bytes 7077892
  48.2 0.7 copy-start.5
  78.8 10.8 %collective-permute-start.6 = (bf16[1,384,32]{1,2,0:T(8,128)(2,1)S(1)}, bf16[1,384,32]{1,2,0:T(8,128)(2,1)S(1)}, u32[]{:S(2)}, u32[]{:S(2)}) collective-permute-start(bf16[1,384,32]{1,2,0:T(8,128)(2,1)S(1)} %slice.242), channel_id=1, source_target_pairs={{0,16},{1,17},{2,18},{3,19},{4,20},{5,21},{6,22},{7,23},{8,24},{9,... | collective-permute-start | bytes 73736 | tf_op jit(solution)/shard_map/ppermute | solution.py:12
  82.0 7.6 %collective-permute-start.7 = (bf16[1,384,32]{1,2,0:T(8,128)(2,1)S(1)}, bf16[1,384,32]{1,2,0:T(8,128)(2,1)S(1)}, u32[]{:S(2)}, u32[]{:S(2)}) collective-permute-start(bf16[1,384,32]{1,2,0:T(8,128)(2,1)S(1)} %slice.244), channel_id=1, source_target_pairs={{16,0},{17,1},{18,2},{19,3},{20,4},{21,5},{22,6},{23,7},{24,8},{25... | collective-permute-start | bytes 73736 | tf_op jit(solution)/shard_map/ppermute | solution.py:15
  86.2 3.8 %copy-start.4 = (bf16[1,3,3,32,32]{4,3,2,1,0:T(8,128)(2,1)S(1)}, bf16[1,3,3,32,32]{4,3,2,1,0:T(8,128)(2,1)}, u32[]{:S(2)}) copy-start(bf16[1,3,3,32,32]{4,3,2,1,0:T(8,128)(2,1)} %param.12) | copy-start | bytes 55300
  91.8 0.7 copy-start.7
where the time goes:
time: 94.2 us; the launch traced here: 93.5 us
  local copies, waits for them, and re-layouts  30.4 us (32%)
  starting transfers between devices  18.9 us (20%)
  blocking collectives  17.8 us (19%)
  matrix products  12.2 us (13%)
  waiting for transfers between devices  7.24 us (8%)
  other arithmetic  6.36 us (7%)
    all_to_all x1, blocking collectives, on_device(): lax.all_to_all(layer_two, 'col', split_axis=2, concat_axis=1, tiled=True)  17.8 us
    slice x9, local copies, waits for them, and re-layouts, conv_taps(): lax.slice(padded, (tap_row, tap_col, 0), (tap_row + stride * (out_rows -...  9.99 us
    all_to_all x3, local copies, waits for them, and re-layouts, on_device(): lax.all_to_all(layer_two, 'col', split_axis=2, concat_axis=1, tiled=True)  9.22 us
    ppermute x3, starting transfers between devices, padded_2(): lax.ppermute(lax.slice_in_dim(block, block.shape[dim] - width, None, axis...  8.97 us
    dot_general x18, matrix products, conv_taps(): jnp.dot(window.reshape(out_rows * out_cols, padded.shape[2]), weight[tap_...  8.73 us
    ppermute x3, waiting for transfers between devices, padded_2(): lax.ppermute(lax.slice_in_dim(block, 0, width, axis=dim), axis, backward)  7.03 us
    unnamed x19, local copies, waits for them, and re-layouts  6.77 us
    ppermute x2, starting transfers between devices, passed_along(): return lax.ppermute(block, axis, route)  5.91 us
  transfers between devices with their start and end apart: 8, of which 3 were waited for; matrix products, arithmetic and copies ran while one was open for 14% of the time, Pallas kernels for 0%

commit v1 on v0

--- a/solution.py
+++ b/solution.py
@@ -58,7 +58,16 @@
     extended = jnp.concatenate([left_column, extended], 1)
     summed = conv_taps(extended, conv_two, tile_rows // 2, tile_cols // 2, 2)
     layer_two = jax.nn.relu(summed + bias_two).astype(jnp.bfloat16)
-    grouped = lax.all_to_all(layer_two, "col", split_axis=2, concat_axis=1, tiled=True)
+
+    def find_rounds_over_axis(piece_in):
+        return jnp.concatenate(
+            lax.all_to_all(
+                jnp.stack(jnp.split(piece_in, lax.axis_size("col"), axis=2), axis=0), "col", 0, 0
+            ),
+            axis=1,
+        )
+
+    grouped = find_rounds_over_axis(layer_two)
     grouped = padded_2(grouped, (("row", 0),), 1)
     grouped = jnp.pad(grouped, ((0, 0), (1, 1), (0, 0)))
     local_groups = conv_three.shape[0]

time: 94.2 us -> 85.5 us (0.908)
  local copies, waits for them, and re-layouts: 30.4 us -> 21.7 us
    all_to_all x3 -> x0, local copies, waits for them, and re-layouts: 9.22 us -> none  [on_device(): lax.all_to_all(layer_two, 'col', split_axis=2, concat_axis=1, tiled=True)]
    reshape x0 -> x2, local copies, waits for them, and re-layouts: none -> 5.87 us  [find_rounds_over_axis(): jnp.concatenate(lax.all_to_all(jnp.stack(jnp.split(piece_in, lax.axis_siz...]
    unnamed x19 -> x36, local copies, waits for them, and re-layouts: 6.77 us -> 4.67 us
    convert_element_type x1 -> x0, local copies, waits for them, and re-layouts: 1.97 us -> none  [on_device(): layer_two = jax.nn.relu(summed + bias_two).astype(jnp.bfloat16)]
    slice x4 -> x3, local copies, waits for them, and re-layouts: 1.37 us -> 0.17 us  [padded_2(): lax.slice_in_dim(block, block.shape[dim] - width, None, axis=dim)]
  transfers between devices with their start and end apart: 8 -> 8, of which waited for: 3 -> 3; matrix products, arithmetic and copies ran while one was open for 14% -> 19% of each run, Pallas kernels for 0% -> 0%
where the time goes in v1:
time: 85.5 us; the launch traced here: 84.9 us
  local copies, waits for them, and re-layouts  21.7 us (25%)
  starting transfers between devices  18.9 us (22%)
  blocking collectives  17.8 us (21%)
  matrix products  12.2 us (14%)
  waiting for transfers between devices  7.24 us (8%)
  other arithmetic  6.36 us (7%)
    all_to_all x1, blocking collectives, find_rounds_over_axis(): lax.all_to_all(jnp.stack(jnp.split(piece_in, lax.axis_size('col'), axis=2...  17.8 us
    slice x9, local copies, waits for them, and re-layouts, conv_taps(): lax.slice(padded, (tap_row, tap_col, 0), (tap_row + stride * (out_rows -...  9.99 us
    ppermute x3, starting transfers between devices, padded_2(): lax.ppermute(lax.slice_in_dim(block, block.shape[dim] - width, None, axis...  8.98 us
    dot_general x18, matrix products, conv_taps(): jnp.dot(window.reshape(out_rows * out_cols, padded.shape[2]), weight[tap_...  8.73 us
    ppermute x3, waiting for transfers between devices, padded_2(): lax.ppermute(lax.slice_in_dim(block, 0, width, axis=dim), axis, backward)  7.03 us
    ppermute x2, starting transfers between devices, passed_along(): return lax.ppermute(block, axis, route)  5.91 us
    reshape x2, local copies, waits for them, and re-layouts, find_rounds_over_axis(): jnp.concatenate(lax.all_to_all(jnp.stack(jnp.split(piece_in, lax.axis_siz...  5.87 us
    concatenate x3, other arithmetic, padded_2(): block = jnp.concatenate([low, block, high], axis=dim)  5.43 us
  transfers between devices with their start and end apart: 8, of which 3 were waited for; matrix products, arithmetic and copies ran while one was open for 19% of the time, Pallas kernels for 0%

profile of v1, /device:TPU:0, one launch (start us, length us, event | category | flops | bytes accessed | tf_op | source)
XLA Modules:
  0.0 84.9 jit_solution(3738763883437311325)
XLA Ops:
  0.0 0.8 fusion.105
  0.8 4.9 %collective-permute-start = (bf16[1,48,256]{2,1,0:T(8,128)(2,1)S(1)}, bf16[1,48,256]{2,1,0:T(8,128)(2,1)S(1)}, u32[]{:S(2)}, u32[]{:S(2)}) collective-permute-start(bf16[1,48,256]{2,1,0:T(8,128)(2,1)S(1)} %get-tuple-element.22), channel_id=1, source_target_pairs={{0,16},{1,17},{2,18},{3,19},{4,20},{5,21},{6,22},{7,23},{8,24},{9,... | collective-permute-start | bytes 73736 | tf_op jit(solution)/shard_map/ppermute | solution.py:12
  5.6 1.3 %collective-permute-start.1 = (bf16[1,48,256]{2,1,0:T(8,128)(2,1)S(1)}, bf16[1,48,256]{2,1,0:T(8,128)(2,1)S(1)}, u32[]{:S(2)}, u32[]{:S(2)}) collective-permute-start(bf16[1,48,256]{2,1,0:T(8,128)(2,1)S(1)} %get-tuple-element.21), channel_id=1, source_target_pairs={{16,0},{17,1},{18,2},{19,3},{20,4},{21,5},{22,6},{23,7},{24,8},{25... | collective-permute-start | bytes 73736 | tf_op jit(solution)/shard_map/ppermute | solution.py:15
  6.9 0.2 collective-permute-done
  7.1 4.2 %collective-permute-done.1 = bf16[1,48,256]{2,1,0:T(8,128)(2,1)S(1)} collective-permute-done((bf16[1,48,256]{2,1,0:T(8,128)(2,1)S(1)}, bf16[1,48,256]{2,1,0:T(8,128)(2,1)S(1)}, u32[]{:S(2)}, u32[]{:S(2)}) %collective-permute-start.1) | collective-permute-done | bytes 24608 | tf_op jit(solution)/shard_map/ppermute | solution.py:15
  11.3 2.2 %pad_maximum_fusion.4 = (bf16[32,48,256]{2,1,0:T(8,128)(2,1)S(1)}, bf16[32,48,256]{2,1,0:T(8,128)(2,1)S(1)}, bf16[34,48,256]{2,1,0:T(8,128)(2,1)S(1)}) fusion(bf16[32,48,256]{2,1,0:T(8,128)(2,1)} %param.7, bf16[1,48,256]{2,1,0:T(8,128)(2,1)S(1)} %collective-permute-done, bf16[1,48,256]{2,1,0:T(8,128)(2,1)S(1)} %collective-permute-done.1, ...), kind=kLoop, calls=%fused_computation.49 | loop fusion | flops 3145728 | bytes 3194880 | tf_op jit(solution)/shard_map/concatenate | solution.py:16
  13.6 1.3 %collective-permute-start.2 = (bf16[34,1,256]{2,1,0:T(2,128)(2,1)S(1)}, bf16[34,1,256]{2,1,0:T(2,128)(2,1)S(1)}, u32[]{:S(2)}, u32[]{:S(2)}) collective-permute-start(bf16[34,1,256]{2,1,0:T(2,128)(2,1)S(1)} %get-tuple-element.16), channel_id=1, source_target_pairs={{0,1},{1,2},{2,3},{3,4},{4,5},{5,6},{6,7},{7,8},{8,9},{9,10},{10,1... | collective-permute-start | bytes 52232 | tf_op jit(solution)/shard_map/ppermute | solution.py:12
  14.9 1.3 %collective-permute-start.3 = (bf16[34,1,256]{2,1,0:T(2,128)(2,1)S(1)}, bf16[34,1,256]{2,1,0:T(2,128)(2,1)S(1)}, u32[]{:S(2)}, u32[]{:S(2)}) collective-permute-start(bf16[34,1,256]{2,1,0:T(2,128)(2,1)S(1)} %get-tuple-element.17), channel_id=1, source_target_pairs={{1,0},{2,1},{3,2},{4,3},{5,4},{6,5},{7,6},{8,7},{9,8},{10,9},{11,1... | collective-permute-start | bytes 52232 | tf_op jit(solution)/shard_map/ppermute | solution.py:15
  16.2 0.4 fusion.54
  16.6 0.4 fusion.47
  17.0 2.8 %collective-permute-done.3 = bf16[34,1,256]{2,1,0:T(2,128)(2,1)S(1)} collective-permute-done((bf16[34,1,256]{2,1,0:T(2,128)(2,1)S(1)}, bf16[34,1,256]{2,1,0:T(2,128)(2,1)S(1)}, u32[]{:S(2)}, u32[]{:S(2)}) %collective-permute-start.3) | collective-permute-done | bytes 17440 | tf_op jit(solution)/shard_map/ppermute | solution.py:15
  19.8 2.9 %pad_maximum_fusion.3 = (bf16[32,48,256]{2,1,0:T(8,128)(2,1)S(1)}, bf16[32,48,256]{2,1,0:T(8,128)(2,1)S(1)}, bf16[32,48,256]{2,1,0:T(8,128)(2,1)S(1)}, bf16[32,4...) fusion(bf16[34,48,256]{2,1,0:T(8,128)(2,1)S(1)} %constant_dynamic-update-slice_fusion,, ...), kind=kLoop, calls=%fused_computation.48 | loop fusion | flops 9437184 | bytes 5588992 | tf_op jit(solution)/shard_map/concatenate | solution.py:16
  22.7 0.4 fusion.45
  23.1 0.4 convolution_add_fusion.5
  23.5 0.4 convolution_add_fusion.4
  23.8 0.4 convolution_add_fusion.3
  24.2 0.7 copy-done.1
  25.0 0.4 convolution_add_fusion.2
  25.3 0.4 convolution_add_fusion.1
  25.7 0.5 fusion.1
  26.2 0.2 copy-done.7
  26.4 0.2 maximum_convert_fusion
  26.6 1.6 %collective-permute-start.4 = (bf16[1,48,256]{2,1,0:T(8,128)(2,1)S(1)}, bf16[1,48,256]{2,1,0:T(8,128)(2,1)S(1)}, u32[]{:S(2)}, u32[]{:S(2)}) collective-permute-start(bf16[1,48,256]{2,1,0:T(8,128)(2,1)S(1)} %slice.272), channel_id=1, source_target_pairs={{0,16},{1,17},{2,18},{3,19},{4,20},{5,21},{6,22},{7,23},{8,24},{9,... | collective-permute-start | bytes 73736 | tf_op jit(solution)/shard_map/ppermute | solution.py:23
  28.2 0.5 slice.231
  28.8 0.5 slice.233
  29.3 0.9 %slice.237 = bf16[16,24,256]{2,1,0:T(8,128)(2,1)S(1)} slice(bf16[32,48,256]{2,1,0:T(8,128)(2,1)S(1)} %maximum_convert_fusion), slice={[1:32:2], [0:47:2], [0:256:1]} | slice | bytes 393216 | tf_op jit(solution)/shard_map/slice | solution.py:30
  30.1 0.9 %slice.239 = bf16[16,24,256]{2,1,0:T(8,128)(2,1)S(1)} slice(bf16[32,48,256]{2,1,0:T(8,128)(2,1)S(1)} %maximum_convert_fusion), slice={[1:32:2], [1:48:2], [0:256:1]} | slice | bytes 393216 | tf_op jit(solution)/shard_map/slice | solution.py:30
  31.1 4.3 %collective-permute-start.5 = (bf16[33,1,256]{2,1,0:T(2,128)(2,1)S(1)}, bf16[33,1,256]{2,1,0:T(2,128)(2,1)S(1)}, u32[]{:S(2)}, u32[]{:S(2)}) collective-permute-start(bf16[33,1,256]{2,1,0:T(2,128)(2,1)S(1)} %fusion.82), channel_id=1, source_target_pairs={{0,1},{1,2},{2,3},{3,4},{4,5},{5,6},{6,7},{7,8},{8,9},{9,10},{10,1... | collective-permute-start | bytes 50696 | tf_op jit(solution)/shard_map/ppermute | solution.py:23
  35.4 0.5 slice.225
  36.0 1.2 %fusion.33 = f32[384,512]{1,0:T(8,128)S(1)} fusion(bf16[384,256]{1,0:T(8,128)(2,1)S(1)} %bitcast.243, bf16[3,3,256,512]{3,2,1,0:T(8,128)(2,1)} %param.10), kind=kOutput, calls=%fused_computation.76 | convolution fusion | flops 100663296 | bytes 1245184 | tf_op jit(solution)/shard_map/dot_general | solution.py:40
  37.2 5.0 %slice.227 = bf16[16,24,256]{2,1,0:T(8,128)(2,1)} slice(bf16[33,48,256]{2,1,0:T(8,128)(2,1)S(1)} %pad_maximum_fusion), slice={[0:31:2], [1:48:2], [0:256:1]} | slice | bytes 393216 | tf_op jit(solution)/shard_map/slice | solution.py:30
  42.2 0.5 maximum_maximum_fusion
  42.7 0.5 slice.223
  43.2 0.5 slice.229
  43.7 0.7 slice.235
  44.5 1.4 %convolution_add_fusion.20 = f32[384,512]{1,0:T(8,128)S(1)} fusion(f32[384,512]{1,0:T(8,128)S(1)} %fusion.33, bf16[384,256]{1,0:T(8,128)(2,1)S(1)} %bitcast.251, bf16[3,3,256,512]{3,2,1,0:T(8,128)(2,1)} %param.10), kind=kOutput, calls=%fused_computation.32 | convolution fusion | flops 100859904 | bytes 2031616 | tf_op jit(solution)/shard_map/dot_general | solution.py:40
  45.9 1.2 %convolution_add_fusion.19 = f32[384,512]{1,0:T(8,128)S(1)} fusion(f32[384,512]{1,0:T(8,128)S(1)} %convolution_add_fusion.20, bf16[384,256]{1,0:T(8,128)(2,1)S(1)} %bitcast.248, bf16[3,3,256,512]{3,2,1,0:T(8,128)(2,1)} %param.10), kind=kOutput, calls=%fused_computation.31 | convolution fusion | flops 100859904 | bytes 2031616 | tf_op jit(solution)/shard_map/dot_general | solution.py:40
  47.1 0.3 convolution_add_fusion.18
  47.4 0.3 convolution_add_fusion.17
  47.6 0.3 convolution_add_fusion.16
  47.9 0.3 convolution_add_fusion.15
  48.2 0.3 convolution_add_fusion.14
  48.4 0.3 convolution_add_fusion.13
  48.7 0.1 copy-done.6
  49.0 0.1 fusion.80
  49.1 0.1 fusion.79
  49.2 0.1 fusion.78
  50.5 1.5 %reshape.196 = bf16[16,2,6144]{2,1,0:T(2,128)(2,1)S(1)} reshape(bf16[16,16,24,32]{3,2,1,0:T(8,128)(2,1)S(1)} %fusion.66) | data formatting | bytes 786432
  52.0 17.8 %all_to_all.5 = bf16[16,2,6144]{2,1,0:T(2,128)(2,1)S(1)} all-to-all(bf16[16,2,6144]{2,1,0:T(2,128)(2,1)S(1)} %reshape.196), channel_id=1, replica_groups=mesh['row'=2,'col'=16] {'col'}, dimensions={0} | all-to-all | bytes 786432 | tf_op jit(solution)/shard_map/all_to_all | solution.py:64
  69.8 0.8 reshape.197
  70.7 2.8 %collective-permute-start.6 = (bf16[1,384,32]{1,2,0:T(8,128)(2,1)S(1)}, bf16[1,384,32]{1,2,0:T(8,128)(2,1)S(1)}, u32[]{:S(2)}, u32[]{:S(2)}) collective-permute-start(bf16[1,384,32]{1,2,0:T(8,128)(2,1)S(1)} %copy.57), channel_id=1, source_target_pairs={{0,16},{1,17},{2,18},{3,19},{4,20},{5,21},{6,22},{7,23},{8,24},{9,... | collective-permute-start | bytes 73736 | tf_op jit(solution)/shard_map/ppermute | solution.py:12
  73.6 1.5 %collective-permute-start.7 = (bf16[1,384,32]{1,2,0:T(8,128)(2,1)S(1)}, bf16[1,384,32]{1,2,0:T(8,128)(2,1)S(1)}, u32[]{:S(2)}, u32[]{:S(2)}) collective-permute-start(bf16[1,384,32]{1,2,0:T(8,128)(2,1)S(1)} %copy.58), channel_id=1, source_target_pairs={{16,0},{17,1},{18,2},{19,3},{20,4},{21,5},{22,6},{23,7},{24,8},{25... | collective-permute-start | bytes 73736 | tf_op jit(solution)/shard_map/ppermute | solution.py:15
  75.1 3.6 %copy.46 = bf16[16,16,24,32]{2,1,3,0:T(8,128)(2,1)S(1)} copy(bf16[16,16,24,32]{3,2,0,1:T(8,128)(2,1)} %bitcast.231) | data formatting | bytes 786432 | tf_op jit(solution)/shard_map/reshape | solution.py:63
  78.7 2.3 %reshape.171 = bf16[16,384,32]{1,2,0:T(8,128)(2,1)S(1)} reshape(bf16[16,16,24,32]{2,1,3,0:T(8,128)(2,1)S(1)} %copy.46) | data formatting | bytes 786432 | tf_op jit(solution)/shard_map/reshape | solution.py:63
  81.0 0.3 fusion.15
  81.4 0.3 fusion.16
  81.7 0.3 fusion.23
  82.0 0.3 convolution_add_fusion.12
  82.3 0.3 convolution_add_fusion.11
  82.6 0.3 convolution_add_fusion.10
  82.9 0.3 convolution_add_fusion.9
  83.2 0.3 convolution_add_fusion.8
  83.5 0.3 convolution_add_fusion.7
  83.9 1.0 %fusion.5 = bf16[16,32,384]{2,1,0:T(8,128)(2,1)} fusion(f32[16,384,32]{1,2,0:T(8,128)S(1)} %fusion.16, f32[16,384,32]{1,2,0:T(8,128)S(1)} %convolution_add_fusion.7, bf16[1,384,32]{1,2,0:T(8,128)(2,1)S(1)} %collective-permute-done.7, bf16[16,384,32]{1,2,0:T(8,128)(2,1)S(1)} %reshape.171, f32[32]{0:T(128)S(1)} %copy-done.8, ...), kind=kOutput, calls=%fused_computation.33 | convolution fusion | flops 14155776 | bytes 2392576 | tf_op jit(solution)/shard_map/rwgi,gio->rgow/dot_general | solution.py:83
  (43 shorter events, 1.7 us)
Async XLA Ops:
  0.8 6.4 %collective-permute-start = (bf16[1,48,256]{2,1,0:T(8,128)(2,1)S(1)}, bf16[1,48,256]{2,1,0:T(8,128)(2,1)S(1)}, u32[]{:S(2)}, u32[]{:S(2)}) collective-permute-start(bf16[1,48,256]{2,1,0:T(8,128)(2,1)S(1)} %get-tuple-element.22), channel_id=1, source_target_pairs={{0,16},{1,17},{2,18},{3,19},{4,20},{5,21},{6,22},{7,23},{8,24},{9,... | collective-permute-start | bytes 73736 | tf_op jit(solution)/shard_map/ppermute | solution.py:12
  5.6 5.7 %collective-permute-start.1 = (bf16[1,48,256]{2,1,0:T(8,128)(2,1)S(1)}, bf16[1,48,256]{2,1,0:T(8,128)(2,1)S(1)}, u32[]{:S(2)}, u32[]{:S(2)}) collective-permute-start(bf16[1,48,256]{2,1,0:T(8,128)(2,1)S(1)} %get-tuple-element.21), channel_id=1, source_target_pairs={{16,0},{17,1},{18,2},{19,3},{20,4},{21,5},{22,6},{23,7},{24,8},{25... | collective-permute-start | bytes 73736 | tf_op jit(solution)/shard_map/ppermute | solution.py:15
  7.1 9.1 %copy-start.3 = (bf16[3,3,256,256]{3,2,1,0:T(8,128)(2,1)S(1)}, bf16[3,3,256,256]{3,2,1,0:T(8,128)(2,1)}, u32[]{:S(2)}) copy-start(bf16[3,3,256,256]{3,2,1,0:T(8,128)(2,1)} %param.8) | copy-start | bytes 3538948
  13.6 3.3 %collective-permute-start.2 = (bf16[34,1,256]{2,1,0:T(2,128)(2,1)S(1)}, bf16[34,1,256]{2,1,0:T(2,128)(2,1)S(1)}, u32[]{:S(2)}, u32[]{:S(2)}) collective-permute-start(bf16[34,1,256]{2,1,0:T(2,128)(2,1)S(1)} %get-tuple-element.16), channel_id=1, source_target_pairs={{0,1},{1,2},{2,3},{3,4},{4,5},{5,6},{6,7},{7,8},{8,9},{9,10},{10,1... | collective-permute-start | bytes 52232 | tf_op jit(solution)/shard_map/ppermute | solution.py:12
  14.9 4.9 %collective-permute-start.3 = (bf16[34,1,256]{2,1,0:T(2,128)(2,1)S(1)}, bf16[34,1,256]{2,1,0:T(2,128)(2,1)S(1)}, u32[]{:S(2)}, u32[]{:S(2)}) collective-permute-start(bf16[34,1,256]{2,1,0:T(2,128)(2,1)S(1)} %get-tuple-element.17), channel_id=1, source_target_pairs={{1,0},{2,1},{3,2},{4,3},{5,4},{6,5},{7,6},{8,7},{9,8},{10,9},{11,1... | collective-permute-start | bytes 52232 | tf_op jit(solution)/shard_map/ppermute | solution.py:15
  23.8 1.1 %copy-start.1 = (bf16[32,48,256]{2,1,0:T(8,128)(2,1)S(1)}, bf16[32,48,256]{2,1,0:T(8,128)(2,1)}, u32[]{:S(2)}) copy-start(bf16[32,48,256]{2,1,0:T(8,128)(2,1)} %param.7) | copy-start | bytes 2359300
  25.7 0.7 copy-start.7
  26.6 4.4 %collective-permute-start.4 = (bf16[1,48,256]{2,1,0:T(8,128)(2,1)S(1)}, bf16[1,48,256]{2,1,0:T(8,128)(2,1)S(1)}, u32[]{:S(2)}, u32[]{:S(2)}) collective-permute-start(bf16[1,48,256]{2,1,0:T(8,128)(2,1)S(1)} %slice.272), channel_id=1, source_target_pairs={{0,16},{1,17},{2,18},{3,19},{4,20},{5,21},{6,22},{7,23},{8,24},{9,... | collective-permute-start | bytes 73736 | tf_op jit(solution)/shard_map/ppermute | solution.py:23
  31.1 11.1 %collective-permute-start.5 = (bf16[33,1,256]{2,1,0:T(2,128)(2,1)S(1)}, bf16[33,1,256]{2,1,0:T(2,128)(2,1)S(1)}, u32[]{:S(2)}, u32[]{:S(2)}) collective-permute-start(bf16[33,1,256]{2,1,0:T(2,128)(2,1)S(1)} %fusion.82), channel_id=1, source_target_pairs={{0,1},{1,2},{2,3},{3,4},{4,5},{5,6},{6,7},{7,8},{8,9},{9,10},{10,1... | collective-permute-start | bytes 50696 | tf_op jit(solution)/shard_map/ppermute | solution.py:23
  42.7 3.2 %copy-start.4 = (bf16[16,24,256]{2,1,0:T(8,128)(2,1)S(1)}, bf16[16,24,256]{2,1,0:T(8,128)(2,1)}, u32[]{:S(2)}) copy-start(bf16[16,24,256]{2,1,0:T(8,128)(2,1)} %slice.227) | copy-start | bytes 589828
  44.5 2.6 %copy-start.2 = (bf16[3,3,256,512]{3,2,1,0:T(8,128)(2,1)S(1)}, bf16[3,3,256,512]{3,2,1,0:T(8,128)(2,1)}, u32[]{:S(2)}) copy-start(bf16[3,3,256,512]{3,2,1,0:T(8,128)(2,1)} %param.10) | copy-start | bytes 7077892
  48.2 0.7 copy-start.6
  70.6 3.1 %copy-start = (bf16[16,16,24,32]{3,2,1,0:T(8,128)(2,1)}, bf16[16,16,24,32]{3,2,1,0:T(8,128)(2,1)S(1)}, u32[]{:S(2)}) copy-start(bf16[16,16,24,32]{3,2,1,0:T(8,128)(2,1)S(1)} %reshape.197) | copy-start | bytes 1179652
  70.7 10.3 %collective-permute-start.6 = (bf16[1,384,32]{1,2,0:T(8,128)(2,1)S(1)}, bf16[1,384,32]{1,2,0:T(8,128)(2,1)S(1)}, u32[]{:S(2)}, u32[]{:S(2)}) collective-permute-start(bf16[1,384,32]{1,2,0:T(8,128)(2,1)S(1)} %copy.57), channel_id=1, source_target_pairs={{0,16},{1,17},{2,18},{3,19},{4,20},{5,21},{6,22},{7,23},{8,24},{9,... | collective-permute-start | bytes 73736 | tf_op jit(solution)/shard_map/ppermute | solution.py:12
  73.6 7.4 %collective-permute-start.7 = (bf16[1,384,32]{1,2,0:T(8,128)(2,1)S(1)}, bf16[1,384,32]{1,2,0:T(8,128)(2,1)S(1)}, u32[]{:S(2)}, u32[]{:S(2)}) collective-permute-start(bf16[1,384,32]{1,2,0:T(8,128)(2,1)S(1)} %copy.58), channel_id=1, source_target_pairs={{16,0},{17,1},{18,2},{19,3},{20,4},{21,5},{22,6},{23,7},{24,8},{25... | collective-permute-start | bytes 73736 | tf_op jit(solution)/shard_map/ppermute | solution.py:15
  78.7 2.7 %copy-start.5 = (bf16[1,3,3,32,32]{4,3,2,1,0:T(8,128)(2,1)S(1)}, bf16[1,3,3,32,32]{4,3,2,1,0:T(8,128)(2,1)}, u32[]{:S(2)}) copy-start(bf16[1,3,3,32,32]{4,3,2,1,0:T(8,128)(2,1)} %param.12) | copy-start | bytes 55300
  83.2 0.7 copy-start.8
